TPU v7x, 1024 devices: a whole 8x8x8 slice. The times are simulated.
1024 devices in a mesh: dp: 64 (over z, x_lo, core), fsdp: 16 (over x_hi, y).
Axes of the slice: x: 8 (x_hi: 2, x_lo: 4; x = x_hi * 4 + x_lo), y: 8, z: 8, core: 2. Of those that a mesh axis runs over, the one named last changes fastest.
Arguments:
- patches: bfloat16 [262144, 384], P(('dp', 'fsdp')), may hold values from -24 to 24
- grad_embed: bfloat16 [262144, 3072], P(('dp', 'fsdp')), may hold values from -6 to 6
- weight: bfloat16 [384, 3072], P(None, 'fsdp'), may hold values from -0.3125 to 0.3125
- straggler: int32 [64], P('dp'), may hold values 0 or 1
- decode: int32 [64], P('dp'), may hold values from 1 to 3
- encode: int32 [64, 2], P('dp'), may hold values from 1 to 3
Outputs:
- embedded: bfloat16 [262144, 3072], P(('dp', 'fsdp'))
- weight_grad: float32 [384, 3072], P('dp', 'fsdp')
All inputs are finite; a program needn't handle non-finite values. No bound on the sum of `straggler` on one device may be relied on, other than what follows from the above.
Results may differ from a plain program's by a relative error of at most 0.001.
Values may be sent and summed in bfloat16 or wider, within the bound.
A program may use at most 32 MiB of HBM per device.

v0:
```python
import jax
import jax.numpy as jnp
from jax import lax
from jax.sharding import PartitionSpec as P


def shifted(block, axis, distance):
    devices = range(lax.axis_size(axis))
    route = [((i - distance) % len(devices), i) for i in devices]
    return lax.ppermute(block, axis, route)


def body(patches, grad_embed, weight, straggler, decode, encode):
    served = straggler * decode
    first_share = served * encode[:, 0]
    second_share = served * encode[:, 1]
    carried = shifted(second_share, "dp", 1)
    count_fsdp = lax.axis_size("fsdp")
    tokens_here = patches.shape[0]
    scale = (first_share + carried)[0].astype(jnp.float32) / (tokens_here * count_fsdp)
    embedded = jnp.dot(
        patches,
        lax.all_gather(weight, "fsdp", axis=1, tiled=True),
        preferred_element_type=jnp.float32,
    ).astype(jnp.bfloat16)
    term = lax.dot_general(
        grad_embed, patches, (((0,), (0,)), ((), ())), preferred_element_type=jnp.float32
    )
    partial_value = lax.psum_scatter(scale * term, "fsdp", scatter_dimension=0, tiled=True)
    upright = partial_value.T
    decoded = lax.psum_scatter(upright, "dp", scatter_dimension=0, tiled=True)
    return (embedded, decoded)


def solution(mesh):
    return jax.shard_map(
        body,
        mesh=mesh,
        in_specs=(
            P(("dp", "fsdp"), None),
            P(("dp", "fsdp"), None),
            P(None, "fsdp"),
            P("dp"),
            P("dp"),
            P("dp", None),
        ),
        out_specs=(P(("dp", "fsdp"), None), P("dp", "fsdp")),
        check_vma=False,
    )
```

profile of v0, /device:TPU:1, one launch (start us, length us, event | category | flops | bytes accessed | tf_op | source)
XLA Modules:
  0.0 909.6 jit_solution(7692540130688939423)
XLA Ops:
  7.2 0.0 copy-start
  7.2 0.0 reduce-scatter.3.cloned.1.call-start
  8.6 1.3 fusion
  10.6 5.2 collective-permute-start
  16.5 10.9 %collective-permute-done = s32[1]{0:T(128)} collective-permute-done((s32[1]{0:T(128)}, s32[1]{0:T(128)}, u32[]{:S(2)}, u32[]{:S(2)}) %collective-permute-start) | collective-permute-done | bytes 36 | tf_op jit(solution)/shard_map/ppermute | solution.py:10
  28.0 0.0 copy-done
  28.0 4.1 broadcast_multiply_fusion
  32.1 0.0 copy-start.1
  32.1 0.0 reduce-scatter.3.cloned.1.call-update
  32.1 0.0 all-gather.2.cloned.1.call-start
  32.1 0.7 all-gather.2.cloned.1.call-update
  32.8 0.0 all-reduce.3.cloned.1.call-start
  32.9 1.3 dynamic-slice
  34.8 238.9 %reduce-scatter.3.cloned.1.call-done = f32[192,384]{1,0:T(8,128)} async-done(((f32[3072,384]{1,0:T(8,128)}), f32[192,384]{1,0:T(8,128)}) %reduce-scatter.3.cloned.1.call-update) | async-done | bytes 294928 | tf_op jit(solution)/shard_map/reduce_scatter | solution.py:29
  273.7 0.0 all-reduce.3.cloned.1.call-update
  273.7 114.9 %all-gather.2.cloned.1.call-done = bf16[384,3072]{0,1:T(8,128)(2,1)} async-done(((bf16[384,192]{0,1:T(8,128)(2,1)}), bf16[384,3072]{0,1:T(8,128)(2,1)}) %all-gather.2.cloned.1.call-update) | async-done | bytes 2359312 | tf_op jit(solution)/shard_map/all_gather | solution.py:23
  388.6 0.0 copy-done.1
  388.6 3.8 convolution_convert_fusion
  392.4 508.9 %all-reduce.3.cloned.1.call-done = f32[384,192]{0,1:T(8,128)} async-done(((f32[384,192]{0,1:T(8,128)}), f32[384,192]{0,1:T(8,128)}) %all-reduce.3.cloned.1.call-update) | async-done | bytes 294928
  901.4 1.0 constant_dynamic-slice_fusion
  902.4 0.7 copy.9
Async XLA Ops:
  7.2 20.8 %copy-start = (bf16[256,3072]{1,0:T(8,128)(2,1)S(1)}, bf16[256,3072]{1,0:T(8,128)(2,1)}, u32[]{:S(2)}) copy-start(bf16[256,3072]{1,0:T(8,128)(2,1)} %param.7) | copy-start | bytes 4718596
  7.2 266.5 %reduce-scatter.3.cloned.1.call-start = ((), (), s32[]{:S(2)}) async-start(), calls=%async_computation.2 | async-start | bytes 5013504 | tf_op jit(solution)/shard_map/reduce_scatter | solution.py:29
  10.6 16.8 %collective-permute-start = (s32[1]{0:T(128)}, s32[1]{0:T(128)}, u32[]{:S(2)}, u32[]{:S(2)}) collective-permute-start(s32[1]{0:T(128)} %mul.17), channel_id=1, source_target_pairs={{1008,0},{0,16},{16,32},{32,48},{48,64},{64,80},{80,96},{96,112},{... | collective-permute-start | bytes 20 | tf_op jit(solution)/shard_map/ppermute | solution.py:10
  32.1 356.6 %copy-start.1 = (bf16[256,384]{1,0:T(8,128)(2,1)S(1)}, bf16[256,384]{1,0:T(8,128)(2,1)}, u32[]{:S(2)}) copy-start(bf16[256,384]{1,0:T(8,128)(2,1)} %param.6) | copy-start | bytes 589828
  32.1 356.5 %all-gather.2.cloned.1.call-start = ((), (), s32[]{:S(2)}) async-start(), calls=%async_computation.1 | async-start | bytes 2506752 | tf_op jit(solution)/shard_map/all_gather | solution.py:23
  32.8 868.5 %all-reduce.3.cloned.1.call-start = ((), (), s32[]{:S(2)}) async-start(), calls=%async_computation.3 | async-start | bytes 589824
Sparse Core Ops, SparseCore 0:
  32.2 241.4 reduce-scatter.2
  278.8 109.7 all-gather.1
  392.5 508.7 all-reduce.2
where the time goes:
time: 910 us
  waiting for transfers between devices  874 us (96%)
  between operations  17.7 us (2%)
    unnamed x4, waiting for transfers between devices  510 us
    reduce_scatter x1, waiting for transfers between devices, body(): lax.psum_scatter(scale * term, 'fsdp', scatter_dimension=0, tiled=True)  239 us
    all_gather x1, waiting for transfers between devices, body(): lax.all_gather(weight, 'fsdp', axis=1, tiled=True)  115 us
  transfers between devices with their start and end apart: 4, of which 4 were waited for; matrix products, arithmetic and copies ran while one was open for 1% of the time, Pallas kernels for 0%

commit v1 on v0

v1 whole, which is shorter than its diff:
```python
import jax
import jax.numpy as jnp
from jax import lax
from jax.experimental import pallas as pl
from jax.experimental.pallas import tpu as pltpu
from jax.sharding import PartitionSpec as P

MESH = pl.DeviceIdType.MESH
F32 = jnp.float32
BF16 = jnp.bfloat16
RING = 8
X_LO = 4
P_SIZE = 384
DW = 3072
TOK = 256
SHARD = DW // 16
HALF = SHARD // 2
COLS = 2 * SHARD
PIECE = 96
PH = PIECE // 2
PLUS, MINUS = 0, 1
STEP = (1, -1)


def hops(first, way):
    return 4 if (first == 0) == (way == PLUS) else 3


def kernel(strag, decode, encode, p_hbm, g_hbm, w_hbm, emb_hbm, out_ref,
           g, p, gsib, psib, wt, t, r1, s, s2, r2, u, s3, r3, emb, ptb, msg, msgs,
           lsem, msem_s, msem_r, tsem_s, tsem_r, xsem_s, xsem_r, asem_s, asem_r, bsem_s, bsem_r,
           sem1_s, sem1_r, sem2_s, sem2_r, sem3_s, sem3_r):
    dp, fs = lax.axis_index("dp"), lax.axis_index("fsdp")
    core = lax.rem(dp, 2)
    xl = lax.rem(lax.div(dp, 2), X_LO)
    z = lax.div(dp, 2 * X_LO)
    xh = lax.div(fs, RING)
    y = lax.rem(fs, RING)
    x = xh * X_LO + xl

    def wrap(v):
        return lax.rem(v + RING, RING)

    def dev(x_, y_, z_, c_):
        return (z_ * 2 * X_LO + lax.rem(x_, X_LO) * 2 + c_, lax.div(x_, X_LO) * RING + y_)

    sib = (dp + 1 - 2 * core, fs)
    chip = lax.div(dp, 2)
    chips = 32
    following = lax.rem(chip + 1, chips)
    preceding = lax.rem(chip + chips - 1, chips)

    def remote(src, dst, ss, rs, to):
        return pltpu.make_async_remote_copy(src_ref=src, dst_ref=dst, send_sem=ss, recv_sem=rs,
                                            device_id=to, device_id_type=MESH)

    shard_rows = pl.ds(pl.multiple_of(fs * SHARD, SHARD), SHARD)
    load_w = pltpu.make_async_copy(w_hbm, wt.at[shard_rows], lsem.at[0])
    load_p = pltpu.make_async_copy(p_hbm, p, lsem.at[1])
    load_g = pltpu.make_async_copy(g_hbm, g, lsem.at[2])
    load_w.start()
    load_p.start()
    load_g.start()

    barrier = pltpu.get_barrier_semaphore()
    partners = [sib]
    for k in range(1, RING):
        partners.append(dev(wrap(x + k - RING), y, z, core))
        partners.append(dev(x, y, wrap(z + k - RING), core))
        partners.append(dev(x, wrap(y + k - RING), z, core))
        partners.append(dev(x, wrap(y + k - RING), z, 1 - core))
    for other in (following, preceding):
        partners.append((2 * other, fs))
        partners.append((2 * other + 1, fs))
    for to in partners:
        pl.semaphore_signal(barrier, inc=1, device_id=to, device_id_type=MESH)

    served = strag[0] * decode[0]
    row = lax.broadcasted_iota(jnp.int32, (8, 128), 0)
    msg[...] = jnp.where(row == 0, served * encode[0, 0], served * encode[0, 1])

    pl.semaphore_wait(barrier, len(partners))

    share_sib = remote(msg, msgs.at[0], msem_s.at[0], msem_r.at[0], sib)
    share_sib.start()
    share_next = [remote(msg, msgs.at[1], msem_s.at[1 + c], msem_r.at[1], (2 * following + c, fs)) for c in (0, 1)]

    @pl.when(core == 1)
    def _():
        for copy in share_next:
            copy.start()

    def unit(x_hi, y_, c_):
        return wt.at[pl.ds(pl.multiple_of((x_hi * RING + y_) * SHARD + c_ * HALF, 32), HALF)]

    xh_of = (xh, 1 - xh)

    def gather_send(kind, way, hop):
        block = unit(xh_of[kind], wrap(y - STEP[way] * hop), core)
        to = dev(x, wrap(y + STEP[way]), z, core)
        return remote(block, block, asem_s.at[kind, way, hop], asem_r.at[kind, way, hop], to)

    def gather_wait(kind, way, hop):
        block = unit(xh_of[kind], wrap(y - STEP[way] * hop), core)
        remote(block, block, asem_s.at[kind, way, hop - 1], asem_r.at[kind, way, hop - 1], sib).wait_recv()

    def pass_on(kind, way, hop, c_):
        block = unit(xh_of[kind], wrap(y - STEP[way] * hop), c_)
        return remote(block, block, bsem_s.at[kind, way, hop], bsem_r.at[kind, way, hop], sib)

    load_w.wait()
    edge = (xl == 0) | (xl == X_LO - 1)
    outward = jnp.where(xl == 0, RING - 1, 1)
    own_unit = unit(xh, y, core)
    cross = [remote(own_unit, own_unit, xsem_s.at[k], xsem_r.at[0],
                    dev(lax.rem(x + (k + 1) * outward, RING), y, z, core)) for k in (0, 1)]

    @pl.when(edge)
    def _():
        for copy in cross:
            copy.start()

    for way in (PLUS, MINUS):
        gather_send(0, way, 0).start()

    load_g.wait()
    load_p.wait()
    tokens = [remote(p, psib, tsem_s.at[2], tsem_r.at[2], sib)]
    for h in (0, 1):
        theirs = pl.ds(pl.multiple_of(h * (DW // 2) + (1 - core) * 2 * COLS, COLS), 2 * COLS)
        tokens.append(remote(g.at[:, theirs], gsib.at[h], tsem_s.at[h], tsem_r.at[h], sib))
    for copy in tokens:
        copy.start()

    feature = lax.broadcasted_iota(jnp.int32, (P_SIZE, P_SIZE), 1)
    twelfth = jnp.right_shift(feature * 43691, 19)
    z_of = jnp.right_shift(feature * 10923, 19)
    place = (twelfth - X_LO * z_of) * PIECE + z_of * 12 + (feature - 12 * twelfth)
    out_row = lax.broadcasted_iota(jnp.int32, (P_SIZE, P_SIZE), 0)
    turn = (
        (out_row == feature).astype(F32).astype(BF16),
        (out_row == place).astype(F32).astype(BF16),
    )

    def features_first(q, tok):
        return lax.dot_general(turn[q], tok, (((1,), (1,)), ((), ())), preferred_element_type=F32).astype(BF16)

    mine = [features_first(q, p[...]) for q in (0, 1)]
    for q in (0, 1):
        ptb[q] = mine[q]

    share_sib.wait_recv()
    remote(msg, msgs.at[1], msem_s.at[1], msem_r.at[1], sib).wait_recv()
    before = msgs[1, 1:2, 0:1]
    first_own, second_own = msg[0:1, 0:1], msg[1:2, 0:1]
    first_sib, second_sib = msgs[0, 0:1, 0:1], msgs[0, 1:2, 0:1]
    lower = core == 0
    scale_own = (first_own + jnp.where(lower, before, second_sib)).astype(F32) / (TOK * 16)
    scale_sib = (first_sib + jnp.where(lower, second_own, before)).astype(F32) / (TOK * 16)

    for copy in tokens:
        copy.wait_recv()
    theirs_t = [features_first(q, psib[...]) for q in (0, 1)]

    pos = (z, x)

    def beside(q, v):
        return dev(x, y, v, core) if q == 0 else dev(v, y, z, core)

    def along(q, h, way, hop):
        n = hops(h, way)
        piece = wrap(pos[q] + STEP[way] * (n - hop))
        src = t.at[q, piece, pl.ds(h * PH, PH)] if hop == 0 else r1.at[q, h, way, hop - 1]
        return piece, remote(src, r1.at[q, h, way, hop], sem1_s.at[q, h, way, hop], sem1_r.at[q, h, way, hop],
                             beside(q, wrap(pos[q] + STEP[way])))

    def along_wait(q, h, way, hop):
        slot = r1.at[q, h, way, hop]
        remote(slot, slot, sem1_s.at[q, h, way, hop], sem1_r.at[q, h, way, hop], sib).wait_recv()

    for q in (0, 1):
        for h in (0, 1):
            here = pl.ds(pl.multiple_of(h * (DW // 2) + core * 2 * COLS + q * COLS, COLS), COLS)
            term = scale_own * jnp.dot(ptb[q], g[:, here], preferred_element_type=F32)
            term += scale_sib * jnp.dot(theirs_t[q], gsib[h, :, q * COLS:(q + 1) * COLS], preferred_element_type=F32)
            if q == 0:
                for k in range(RING):
                    t[0, k, h * PH:(h + 1) * PH, :] = term[k * PH:(k + 1) * PH]
                for way in (PLUS, MINUS):
                    along(0, h, way, 0)[1].start()
            else:
                for k in range(X_LO):
                    t[1, h * X_LO + k, :, :] = term[k * PIECE:(k + 1) * PIECE]
    for h in (0, 1):
        for way in (PLUS, MINUS):
            along(1, h, way, 0)[1].start()

    other_unit = unit(1 - xh, y, core)
    remote(other_unit, other_unit, xsem_s.at[0], xsem_r.at[0], sib).wait_recv()
    for way in (MINUS, PLUS):
        gather_send(1, way, 0).start()
    pass_on(1, PLUS, 0, core).start()

    for hop in range(1, 5):
        for h in (0, 1):
            for way in (PLUS, MINUS):
                for q in (0, 1):
                    n = hops(h, way)
                    if hop < n:
                        along_wait(q, h, way, hop - 1)
                        piece, copy = along(q, h, way, hop)
                        slot = r1.at[q, h, way, hop - 1]
                        slot[...] += t[q, piece, h * PH:(h + 1) * PH, :]
                        copy.start()
                if hop <= hops(h, way):
                    gather_wait(h, way, hop)
                    if hop < hops(h, way):
                        gather_send(h, way, hop).start()
                    pass_on(h, way, hop, core).start()

    pos2 = (x, z)

    def across(q, j):
        k = wrap(pos2[q] + j - RING)
        return remote(s2.at[q, k], r2.at[q, j], sem2_s.at[q, j], sem2_r.at[q, j], beside(1 - q, k))

    for q in (0, 1):
        for h in (0, 1):
            for way in (PLUS, MINUS):
                along_wait(q, h, way, hops(h, way) - 1)
            s[q, h * PH:(h + 1) * PH, :] = (
                t[q, pos[q], h * PH:(h + 1) * PH, :]
                + r1[q, h, PLUS, hops(h, PLUS) - 1] + r1[q, h, MINUS, hops(h, MINUS) - 1]
            )
        s[q, PIECE:PIECE + 8, :] = jnp.zeros((8, COLS), F32)
        for k in range(RING):
            s2[q, k] = s[q, 12 * k:12 * k + 16, :]
        for j in range(1, RING):
            across(q, j).start()

    for kind in (0, 1):
        for way in (PLUS, MINUS):
            for hop in range(1, hops(kind, way) + 1):
                pass_on(kind, way, hop, 1 - core).wait_recv()
    pass_on(1, PLUS, 0, 1 - core).wait_recv()

    def embed(j, carry):
        at = pl.multiple_of(j * COLS, COLS)
        e = lax.dot_general(p[...], wt[pl.ds(at, COLS), :], (((1,), (1,)), ((), ())), preferred_element_type=F32)
        emb[:, pl.ds(at, COLS)] = e.astype(BF16)
        return carry

    lax.fori_loop(0, DW // COLS, embed, 0)
    store = pltpu.make_async_copy(emb, emb_hbm, lsem.at[3])
    store.start()

    def onward(q, par, c_):
        y_to = 4 * core + 2 * q + par
        return y_to, remote(s3.at[q, par, c_], r3.at[y], sem3_s.at[q, par, c_], sem3_r.at[y], dev(x, y_to, z, c_))

    for q in (0, 1):
        for j in range(1, RING):
            across(q, j).wait_recv()
        total = s2[q, pos2[q]]
        for j in range(1, RING):
            total += r2[q, j]
        u[q] = total
        for par in (0, 1):
            for c_ in (0, 1):
                s3[q, par, c_] = u[q, 6 * c_:6 * c_ + 8, par * SHARD:(par + 1) * SHARD]
                y_to, copy = onward(q, par, c_)
                self_ = (y_to == y) & (core == c_)

                @pl.when(self_)
                def _():
                    r3[y] = s3[q, par, c_]

                @pl.when(jnp.logical_not(self_))
                def _():
                    copy.start()

    summed_by = lax.div(y, 4)
    for k in range(RING):
        slot = r3.at[k]

        @pl.when(jnp.logical_not((y == k) & (core == summed_by)))
        def _():
            remote(slot, slot, sem3_s.at[0, 0, 0], sem3_r.at[k], sib).wait_recv()

    total = r3[0]
    for k in range(1, RING):
        total += r3[k]
    out_ref[...] = total[0:6]

    share_sib.wait_send()

    @pl.when(core == 1)
    def _():
        for copy in share_next:
            copy.wait_send()

    @pl.when(edge)
    def _():
        for copy in cross:
            copy.wait_send()

    for copy in tokens:
        copy.wait_send()
    pass_on(1, PLUS, 0, core).wait_send()
    for h in (0, 1):
        for way in (PLUS, MINUS):
            for hop in range(hops(h, way)):
                gather_send(h, way, hop).wait_send()
                pass_on(h, way, hop + 1, core).wait_send()
                for q in (0, 1):
                    along(q, h, way, hop)[1].wait_send()
    for q in (0, 1):
        for j in range(1, RING):
            across(q, j).wait_send()
        for par in (0, 1):
            for c_ in (0, 1):
                y_to, copy = onward(q, par, c_)

                @pl.when(jnp.logical_not((y_to == y) & (core == c_)))
                def _():
                    copy.wait_send()
    store.wait()


def body(patches, grad_embed, weight, straggler, decode, encode):
    any_ = pl.BlockSpec(memory_space=pl.ANY)
    smem = pl.BlockSpec(memory_space=pltpu.SMEM)
    dma = pltpu.SemaphoreType.DMA
    return pl.pallas_call(
        kernel,
        out_shape=(
            jax.ShapeDtypeStruct((TOK, DW), BF16),
            jax.ShapeDtypeStruct((6, SHARD), F32),
        ),
        in_specs=[smem, smem, smem, any_, any_, any_],
        out_specs=(any_, pl.BlockSpec(memory_space=pltpu.VMEM)),
        scratch_shapes=[
            pltpu.VMEM((TOK, DW), BF16),
            pltpu.VMEM((TOK, P_SIZE), BF16),
            pltpu.VMEM((2, TOK, 2 * COLS), BF16),
            pltpu.VMEM((TOK, P_SIZE), BF16),
            pltpu.VMEM((DW, P_SIZE), BF16),
            pltpu.VMEM((2, RING, PIECE, COLS), F32),
            pltpu.VMEM((2, 2, 2, 4, PH, COLS), F32),
            pltpu.VMEM((2, PIECE + 8, COLS), F32),
            pltpu.VMEM((2, RING, 16, COLS), F32),
            pltpu.VMEM((2, RING, 16, COLS), F32),
            pltpu.VMEM((2, 16, COLS), F32),
            pltpu.VMEM((2, 2, 2, 8, SHARD), F32),
            pltpu.VMEM((RING, 8, SHARD), F32),
            pltpu.VMEM((TOK, DW), BF16),
            pltpu.VMEM((2, P_SIZE, TOK), BF16),
            pltpu.VMEM((8, 128), jnp.int32),
            pltpu.VMEM((2, 8, 128), jnp.int32),
            dma((4,)),
            dma((3,)), dma((2,)),
            dma((3,)), dma((3,)),
            dma((2,)), dma((1,)),
            dma((2, 2, 4)), dma((2, 2, 4)),
            dma((2, 2, 5)), dma((2, 2, 5)),
            dma((2, 2, 2, 4)), dma((2, 2, 2, 4)),
            dma((2, RING)), dma((2, RING)),
            dma((2, 2, 2)), dma((RING,)),
        ],
        compiler_params=pltpu.CompilerParams(
            collective_id=0, has_side_effects=True, vmem_limit_bytes=48 * 1024 * 1024
        ),
    )(straggler, decode, encode, patches, grad_embed, weight.T)


def solution(mesh):
    return jax.shard_map(
        body,
        mesh=mesh,
        in_specs=(
            P(("dp", "fsdp"), None),
            P(("dp", "fsdp"), None),
            P(None, "fsdp"),
            P("dp"),
            P("dp"),
            P("dp", None),
        ),
        out_specs=(P(("dp", "fsdp"), None), P("dp", "fsdp")),
        check_vma=False,
    )
```

time: 910 us -> 67.6 us (0.07)
  waiting for transfers between devices: 874 us -> 0 us
  Pallas kernels: 0 us -> 59.8 us
  between operations: 17.7 us -> 1.94 us
    unnamed x4 -> x0, waiting for transfers between devices: 510 us -> none
    reduce_scatter x1 -> x0, waiting for transfers between devices: 239 us -> none  [body(): lax.psum_scatter(scale * term, 'fsdp', scatter_dimension=0, tiled=True)]
    all_gather x1 -> x0, waiting for transfers between devices: 115 us -> none  [body(): lax.all_gather(weight, 'fsdp', axis=1, tiled=True)]
    pallas_call x0 -> x1, Pallas kernels: none -> 59.8 us  [body(): pl.pallas_call(kernel, out_shape=(jax.ShapeDtypeStruct((TOK, DW), BF16),...]
    ppermute x1 -> x0, waiting for transfers between devices: 10.9 us -> none  [shifted(): return lax.ppermute(block, axis, route)]
  transfers between devices with their start and end apart: 4 -> 0, of which waited for: 4 -> 0; matrix products, arithmetic and copies ran while one was open for 1% -> 0% of each run, Pallas kernels for 0% -> 0%
where the time goes in v1:
time: 67.6 us; the launch traced here: 67.3 us
  Pallas kernels  59.8 us (88%)
  local copies, waits for them, and re-layouts  5.63 us (8%)
  between operations  1.94 us (3%)
    pallas_call x1, Pallas kernels, body(): pl.pallas_call(kernel, out_shape=(jax.ShapeDtypeStruct((TOK, DW), BF16),...  59.8 us
    unnamed x10, local copies, waits for them, and re-layouts  5.63 us

profile of v1, /device:TPU:1, one launch (start us, length us, event | category | flops | bytes accessed | tf_op | source)
XLA Modules:
  0.0 67.3 jit_solution(3192533019040925460)
XLA Ops:
  1.9 0.0 copy-start
  1.9 1.4 %copy-done = bf16[256,3072]{1,0:T(8,128)(2,1)S(1)} copy-done((bf16[256,3072]{1,0:T(8,128)(2,1)S(1)}, bf16[256,3072]{1,0:T(8,128)(2,1)}, u32[]{:S(2)}) %copy-start) | copy-done | bytes 1572888
  3.3 0.0 copy-start.1
  3.3 0.9 %copy-done.1 = bf16[256,384]{1,0:T(8,128)(2,1)S(1)} copy-done((bf16[256,384]{1,0:T(8,128)(2,1)S(1)}, bf16[256,384]{1,0:T(8,128)(2,1)}, u32[]{:S(2)}) %copy-start.1) | copy-done | bytes 196632
  4.3 0.0 copy-start.2
  4.3 0.9 %copy-done.2 = bf16[384,192]{0,1:T(8,128)(2,1)S(1)} copy-done((bf16[384,192]{0,1:T(8,128)(2,1)S(1)}, bf16[384,192]{0,1:T(8,128)(2,1)}, u32[]{:S(2)}) %copy-start.2) | copy-done | bytes 147480
  5.2 0.0 copy-start.3
  5.2 0.7 copy-done.3
  5.8 59.8 %shard_map.77 = (bf16[256,3072]{1,0:T(8,128)(2,1)S(1)}, f32[6,192]{1,0:T(8,128)S(1)}) custom-call(s32[1]{0:T(128)S(6)} %copy.10.strag, s32[1]{0:T(128)S(6)} %copy.11.decode, s32[1,2]{1,0:T(1,128)S(1)} %copy-done.3, bf16[256,384]{1,0:T(8,128)(2,1)S(1)} %copy-done.1, bf16[256,3072]{1,0:T(8,128)(2,1)S(1)} %copy-done, bf16[192,384]{1,0:T(8,128)(2,1)S(1)} %bitcast.1), custom_call_target="tpu_custom_call" | custom-call | tf_op jit(solution)/shard_map/pallas_call | solution.py:334
  65.6 1.1 %copy.12 = bf16[256,3072]{1,0:T(8,128)(2,1)} copy(bf16[256,3072]{1,0:T(8,128)(2,1)S(1)} %get-tuple-element.4) | data formatting | bytes 3145728
  66.7 0.6 copy.13
Async XLA Ops:
  1.9 1.4 %copy-start = (bf16[256,3072]{1,0:T(8,128)(2,1)S(1)}, bf16[256,3072]{1,0:T(8,128)(2,1)}, u32[]{:S(2)}) copy-start(bf16[256,3072]{1,0:T(8,128)(2,1)} %g_hbm.1) | copy-start | bytes 4718596
  3.3 0.9 %copy-start.1 = (bf16[256,384]{1,0:T(8,128)(2,1)S(1)}, bf16[256,384]{1,0:T(8,128)(2,1)}, u32[]{:S(2)}) copy-start(bf16[256,384]{1,0:T(8,128)(2,1)} %p_hbm.1) | copy-start | bytes 589828
  4.3 0.9 %copy-start.2 = (bf16[384,192]{0,1:T(8,128)(2,1)S(1)}, bf16[384,192]{0,1:T(8,128)(2,1)}, u32[]{:S(2)}) copy-start(bf16[384,192]{0,1:T(8,128)(2,1)} %param.8) | copy-start | bytes 442372
  5.2 0.7 copy-start.3

commit v2 on v1

--- a/solution.py
+++ b/solution.py
@@ -20,14 +20,30 @@
 PH = PIECE // 2
 PLUS, MINUS = 0, 1
 STEP = (1, -1)
+SCALE = 8
+I16 = jnp.int16
 
 
 def hops(first, way):
     return 4 if (first == 0) == (way == PLUS) else 3
 
 
-def kernel(strag, decode, encode, p_hbm, g_hbm, w_hbm, emb_hbm, out_ref,
-           g, p, gsib, psib, wt, t, r1, s, s2, r2, u, s3, r3, emb, ptb, msg, msgs,
+def scales(top):
+    return jnp.floor(jnp.log2(jnp.maximum(top, 2.0 ** -100))) - 14.0
+
+
+def code(v):
+    e = scales(jnp.max(jnp.abs(v), axis=0, keepdims=True))
+    return jnp.clip(jnp.round(v * jnp.exp2(-e)), -32767.0, 32767.0), e
+
+
+def decoded(ref, rows):
+    scale = jnp.exp2(ref[rows:rows + 1, :].astype(jnp.int32).astype(F32))
+    return ref[0:rows, :].astype(jnp.int32).astype(F32) * scale
+
+
+def kernel(strag, decode, enc_hbm, p_hbm, g_hbm, w_hbm, emb, out_ref,
+           encode, g, p, gsib, psib, wt, t, q1, r1, s, s2, r2, u, s3, r3, msg, msgs,
            lsem, msem_s, msem_r, tsem_s, tsem_r, xsem_s, xsem_r, asem_s, asem_r, bsem_s, bsem_r,
            sem1_s, sem1_r, sem2_s, sem2_r, sem3_s, sem3_r):
     dp, fs = lax.axis_index("dp"), lax.axis_index("fsdp")
@@ -58,23 +74,26 @@
     load_w = pltpu.make_async_copy(w_hbm, wt.at[shard_rows], lsem.at[0])
     load_p = pltpu.make_async_copy(p_hbm, p, lsem.at[1])
     load_g = pltpu.make_async_copy(g_hbm, g, lsem.at[2])
+    load_e = pltpu.make_async_copy(enc_hbm, encode, lsem.at[3])
+    load_e.start()
     load_w.start()
     load_p.start()
     load_g.start()
 
     barrier = pltpu.get_barrier_semaphore()
     partners = [sib]
-    for k in range(1, RING):
+    for k in (1, RING - 1):
         partners.append(dev(wrap(x + k - RING), y, z, core))
         partners.append(dev(x, y, wrap(z + k - RING), core))
         partners.append(dev(x, wrap(y + k - RING), z, core))
-        partners.append(dev(x, wrap(y + k - RING), z, 1 - core))
+        partners.append(dev(lax.rem(x + 2 * k, RING), y, z, core))
     for other in (following, preceding):
         partners.append((2 * other, fs))
         partners.append((2 * other + 1, fs))
     for to in partners:
         pl.semaphore_signal(barrier, inc=1, device_id=to, device_id_type=MESH)
 
+    load_e.wait()
     served = strag[0] * decode[0]
     row = lax.broadcasted_iota(jnp.int32, (8, 128), 0)
     msg[...] = jnp.where(row == 0, served * encode[0, 0], served * encode[0, 1])
@@ -145,9 +164,29 @@
     def features_first(q, tok):
         return lax.dot_general(turn[q], tok, (((1,), (1,)), ((), ())), preferred_element_type=F32).astype(BF16)
 
-    mine = [features_first(q, p[...]) for q in (0, 1)]
-    for q in (0, 1):
-        ptb[q] = mine[q]
+    def columns(q, h):
+        return pl.ds(pl.multiple_of(h * (DW // 2) + core * 2 * COLS + q * COLS, COLS), COLS)
+
+    for q in (0, 1):
+        mine = features_first(q, p[...])
+        for h in (0, 1):
+            term = jnp.dot(mine, g[:, columns(q, h)], preferred_element_type=F32)
+            if q == 0:
+                for k in range(RING):
+                    t[0, k, h * PH:(h + 1) * PH, :] = term[k * PH:(k + 1) * PH]
+            else:
+                for k in range(X_LO):
+                    t[1, h * X_LO + k, :, :] = term[k * PIECE:(k + 1) * PIECE]
+
+    def gather_hop(kind, hop):
+        for way in (PLUS, MINUS):
+            if hop <= hops(kind, way):
+                gather_wait(kind, way, hop)
+                if hop < hops(kind, way):
+                    gather_send(kind, way, hop).start()
+                pass_on(kind, way, hop, core).start()
+
+    gather_hop(0, 1)
 
     share_sib.wait_recv()
     remote(msg, msgs.at[1], msem_s.at[1], msem_r.at[1], sib).wait_recv()
@@ -160,7 +199,6 @@
 
     for copy in tokens:
         copy.wait_recv()
-    theirs_t = [features_first(q, psib[...]) for q in (0, 1)]
 
     pos = (z, x)
 
@@ -168,32 +206,41 @@
         return dev(x, y, v, core) if q == 0 else dev(v, y, z, core)
 
     def along(q, h, way, hop):
-        n = hops(h, way)
-        piece = wrap(pos[q] + STEP[way] * (n - hop))
-        src = t.at[q, piece, pl.ds(h * PH, PH)] if hop == 0 else r1.at[q, h, way, hop - 1]
-        return piece, remote(src, r1.at[q, h, way, hop], sem1_s.at[q, h, way, hop], sem1_r.at[q, h, way, hop],
-                             beside(q, wrap(pos[q] + STEP[way])))
+        slot = q1.at[q, h, way, hop]
+        return remote(slot, r1.at[q, h, way, hop], sem1_s.at[q, h, way, hop], sem1_r.at[q, h, way, hop],
+                      beside(q, wrap(pos[q] + STEP[way])))
+
+    def along_send(q, h, way, hop):
+        piece = wrap(pos[q] + STEP[way] * (hops(h, way) - hop))
+        v = t[q, piece, h * PH:(h + 1) * PH, :]
+        if hop:
+            v += decoded(r1.at[q, h, way, hop - 1], PH)
+        v, e = code(v)
+        q1[q, h, way, hop, 0:PH, :] = v.astype(jnp.int32).astype(I16)
+        q1[q, h, way, hop, PH:PH + SCALE, :] = jnp.broadcast_to(e, (SCALE, COLS)).astype(jnp.int32).astype(I16)
+        along(q, h, way, hop).start()
 
     def along_wait(q, h, way, hop):
         slot = r1.at[q, h, way, hop]
         remote(slot, slot, sem1_s.at[q, h, way, hop], sem1_r.at[q, h, way, hop], sib).wait_recv()
 
     for q in (0, 1):
+        others = features_first(q, psib[...])
         for h in (0, 1):
-            here = pl.ds(pl.multiple_of(h * (DW // 2) + core * 2 * COLS + q * COLS, COLS), COLS)
-            term = scale_own * jnp.dot(ptb[q], g[:, here], preferred_element_type=F32)
-            term += scale_sib * jnp.dot(theirs_t[q], gsib[h, :, q * COLS:(q + 1) * COLS], preferred_element_type=F32)
+            term = scale_sib * jnp.dot(others, gsib[h, :, q * COLS:(q + 1) * COLS], preferred_element_type=F32)
             if q == 0:
                 for k in range(RING):
-                    t[0, k, h * PH:(h + 1) * PH, :] = term[k * PH:(k + 1) * PH]
+                    rows = slice(h * PH, (h + 1) * PH)
+                    t[0, k, rows, :] = scale_own * t[0, k, rows, :] + term[k * PH:(k + 1) * PH]
                 for way in (PLUS, MINUS):
-                    along(0, h, way, 0)[1].start()
+                    along_send(0, h, way, 0)
             else:
                 for k in range(X_LO):
-                    t[1, h * X_LO + k, :, :] = term[k * PIECE:(k + 1) * PIECE]
+                    at = h * X_LO + k
+                    t[1, at, :, :] = scale_own * t[1, at, :, :] + term[k * PIECE:(k + 1) * PIECE]
     for h in (0, 1):
         for way in (PLUS, MINUS):
-            along(1, h, way, 0)[1].start()
+            along_send(1, h, way, 0)
 
     other_unit = unit(1 - xh, y, core)
     remote(other_unit, other_unit, xsem_s.at[0], xsem_r.at[0], sib).wait_recv()
@@ -201,22 +248,15 @@
         gather_send(1, way, 0).start()
     pass_on(1, PLUS, 0, core).start()
 
-    for hop in range(1, 5):
+    for hop in range(1, 4):
         for h in (0, 1):
             for way in (PLUS, MINUS):
                 for q in (0, 1):
-                    n = hops(h, way)
-                    if hop < n:
+                    if hop < hops(h, way):
                         along_wait(q, h, way, hop - 1)
-                        piece, copy = along(q, h, way, hop)
-                        slot = r1.at[q, h, way, hop - 1]
-                        slot[...] += t[q, piece, h * PH:(h + 1) * PH, :]
-                        copy.start()
-                if hop <= hops(h, way):
-                    gather_wait(h, way, hop)
-                    if hop < hops(h, way):
-                        gather_send(h, way, hop).start()
-                    pass_on(h, way, hop, core).start()
+                        along_send(q, h, way, hop)
+        gather_hop(0, hop + 1)
+        gather_hop(1, hop)
 
     pos2 = (x, z)
 
@@ -230,13 +270,18 @@
                 along_wait(q, h, way, hops(h, way) - 1)
             s[q, h * PH:(h + 1) * PH, :] = (
                 t[q, pos[q], h * PH:(h + 1) * PH, :]
-                + r1[q, h, PLUS, hops(h, PLUS) - 1] + r1[q, h, MINUS, hops(h, MINUS) - 1]
+                + decoded(r1.at[q, h, PLUS, hops(h, PLUS) - 1], PH) + decoded(r1.at[q, h, MINUS, hops(h, MINUS) - 1], PH)
             )
         s[q, PIECE:PIECE + 8, :] = jnp.zeros((8, COLS), F32)
+    data_row = lax.broadcasted_iota(jnp.int32, (16, COLS), 0) < 12
+    for q in (0, 1):
         for k in range(RING):
-            s2[q, k] = s[q, 12 * k:12 * k + 16, :]
+            v = jnp.where(data_row, s[q, 12 * k:12 * k + 16, :], 0.0)
+            v, e = code(v)
+            s2[q, k] = jnp.where(data_row, v, e).astype(jnp.int32).astype(I16)
         for j in range(1, RING):
             across(q, j).start()
+    gather_hop(1, 4)
 
     for kind in (0, 1):
         for way in (PLUS, MINUS):
@@ -251,8 +296,6 @@
         return carry
 
     lax.fori_loop(0, DW // COLS, embed, 0)
-    store = pltpu.make_async_copy(emb, emb_hbm, lsem.at[3])
-    store.start()
 
     def onward(q, par, c_):
         y_to = 4 * core + 2 * q + par
@@ -261,10 +304,11 @@
     for q in (0, 1):
         for j in range(1, RING):
             across(q, j).wait_recv()
-        total = s2[q, pos2[q]]
+        total = decoded(s2.at[q, pos2[q]], 12)
         for j in range(1, RING):
-            total += r2[q, j]
-        u[q] = total
+            total += decoded(r2.at[q, j], 12)
+        u[q, 0:12, :] = total
+        u[q, 12:16, :] = jnp.zeros((4, COLS), F32)
         for par in (0, 1):
             for c_ in (0, 1):
                 s3[q, par, c_] = u[q, 6 * c_:6 * c_ + 8, par * SHARD:(par + 1) * SHARD]
@@ -313,7 +357,7 @@
                 gather_send(h, way, hop).wait_send()
                 pass_on(h, way, hop + 1, core).wait_send()
                 for q in (0, 1):
-                    along(q, h, way, hop)[1].wait_send()
+                    along(q, h, way, hop).wait_send()
     for q in (0, 1):
         for j in range(1, RING):
             across(q, j).wait_send()
@@ -324,37 +368,37 @@
                 @pl.when(jnp.logical_not((y_to == y) & (core == c_)))
                 def _():
                     copy.wait_send()
-    store.wait()
 
 
 def body(patches, grad_embed, weight, straggler, decode, encode):
-    any_ = pl.BlockSpec(memory_space=pl.ANY)
+    hbm = pl.BlockSpec(memory_space=pltpu.HBM)
+    vmem = pl.BlockSpec(memory_space=pltpu.VMEM)
     smem = pl.BlockSpec(memory_space=pltpu.SMEM)
     dma = pltpu.SemaphoreType.DMA
     return pl.pallas_call(
         kernel,
         out_shape=(
-            jax.ShapeDtypeStruct((TOK, DW), BF16),
-            jax.ShapeDtypeStruct((6, SHARD), F32),
+            pltpu.VMEM((TOK, DW), BF16),
+            pltpu.VMEM((6, SHARD), F32),
         ),
-        in_specs=[smem, smem, smem, any_, any_, any_],
-        out_specs=(any_, pl.BlockSpec(memory_space=pltpu.VMEM)),
+        in_specs=[smem, smem, hbm, hbm, hbm, hbm],
+        out_specs=(vmem, vmem),
         scratch_shapes=[
+            pltpu.SMEM((1, 2), jnp.int32),
             pltpu.VMEM((TOK, DW), BF16),
             pltpu.VMEM((TOK, P_SIZE), BF16),
             pltpu.VMEM((2, TOK, 2 * COLS), BF16),
             pltpu.VMEM((TOK, P_SIZE), BF16),
             pltpu.VMEM((DW, P_SIZE), BF16),
             pltpu.VMEM((2, RING, PIECE, COLS), F32),
-            pltpu.VMEM((2, 2, 2, 4, PH, COLS), F32),
+            pltpu.VMEM((2, 2, 2, 4, PH + SCALE, COLS), I16),
+            pltpu.VMEM((2, 2, 2, 4, PH + SCALE, COLS), I16),
             pltpu.VMEM((2, PIECE + 8, COLS), F32),
-            pltpu.VMEM((2, RING, 16, COLS), F32),
-            pltpu.VMEM((2, RING, 16, COLS), F32),
+            pltpu.VMEM((2, RING, 16, COLS), I16),
+            pltpu.VMEM((2, RING, 16, COLS), I16),
             pltpu.VMEM((2, 16, COLS), F32),
             pltpu.VMEM((2, 2, 2, 8, SHARD), F32),
             pltpu.VMEM((RING, 8, SHARD), F32),
-            pltpu.VMEM((TOK, DW), BF16),
-            pltpu.VMEM((2, P_SIZE, TOK), BF16),
             pltpu.VMEM((8, 128), jnp.int32),
             pltpu.VMEM((2, 8, 128), jnp.int32),
             dma((4,)),
@@ -370,7 +414,7 @@
         compiler_params=pltpu.CompilerParams(
             collective_id=0, has_side_effects=True, vmem_limit_bytes=48 * 1024 * 1024
         ),
-    )(straggler, decode, encode, patches, grad_embed, weight.T)
+    )(straggler, decode, *(pltpu.with_memory_space_constraint(v, pltpu.HBM) for v in (encode, patches, grad_embed, weight.T)))
 
 
 def solution(mesh):

time: 67.6 us -> 59.7 us (0.88)
  Pallas kernels: 59.8 us -> 55.8 us
  local copies, waits for them, and re-layouts: 5.63 us -> 1.74 us
    pallas_call x1, Pallas kernels: 59.8 us -> 55.8 us  [body(): pl.pallas_call(kernel, out_shape=(pltpu.VMEM((TOK, DW), BF16), pltpu.VMEM...]
    unnamed x10 -> x2, local copies, waits for them, and re-layouts: 5.63 us -> 1.74 us
where the time goes in v2:
time: 59.7 us; the launch traced here: 59.5 us
  Pallas kernels  55.8 us (93%)
  between operations  1.93 us (3%)
  local copies, waits for them, and re-layouts  1.74 us (3%)
    pallas_call x1, Pallas kernels, body(): pl.pallas_call(kernel, out_shape=(pltpu.VMEM((TOK, DW), BF16), pltpu.VMEM...  55.8 us
    unnamed x2, local copies, waits for them, and re-layouts  1.74 us

profile of v2, /device:TPU:1, one launch (start us, length us, event | category | flops | bytes accessed | tf_op | source)
XLA Modules:
  0.0 59.5 jit_solution(15110112747781516722)
XLA Ops:
  1.9 55.8 %shard_map.77 = (bf16[256,3072]{1,0:T(8,128)(2,1)S(1)}, f32[6,192]{1,0:T(8,128)S(1)}) custom-call(s32[1]{0:T(128)S(6)} %copy.12.strag, s32[1]{0:T(128)S(6)} %copy.13.decode, s32[1,2]{1,0:T(1,128)} %enc_hbm.1, bf16[256,384]{1,0:T(8,128)(2,1)} %p_hbm.1, bf16[256,3072]{1,0:T(8,128)(2,1)} %g_hbm.1, bf16[192,384]{1,0:T(8,128)(2,1)} %bitcast.1), custom_call_target="tpu_custom_call" | custom-call | tf_op jit(solution)/shard_map/pallas_call | solution.py:378
  57.8 1.1 %copy.10 = bf16[256,3072]{1,0:T(8,128)(2,1)} copy(bf16[256,3072]{1,0:T(8,128)(2,1)S(1)} %get-tuple-element.2) | data formatting | bytes 3145728
  58.9 0.6 %copy.11 = f32[6,192]{1,0:T(8,128)} copy(f32[6,192]{1,0:T(8,128)S(1)} %get-tuple-element.3) | data formatting | bytes 9216

commit v3 on v2

v3 whole, which is shorter than its diff:
```python
import jax
import jax.numpy as jnp
from jax import lax
from jax.experimental import pallas as pl
from jax.experimental.pallas import tpu as pltpu
from jax.sharding import PartitionSpec as P

MESH = pl.DeviceIdType.MESH
F32 = jnp.float32
BF16 = jnp.bfloat16
RING = 8
X_LO = 4
P_SIZE = 384
DW = 3072
TOK = 256
SHARD = DW // 16
HALF = SHARD // 2
COLS = 2 * SHARD
PIECE = 96
PH = PIECE // 2
PLUS, MINUS = 0, 1
STEP = (1, -1)
SCALE = 8
I16 = jnp.int16


OWN_HOPS = (3, 4)
REACH = (1, 2, -1, -2, 3, 4, -3)


def scales(top):
    return jnp.floor(jnp.log2(jnp.maximum(top, 2.0 ** -100))) - 14.0


def code(v, over=0):
    e = scales(jnp.max(jnp.abs(v), axis=over, keepdims=True))
    return jnp.clip(jnp.round(v * jnp.exp2(-e)), -32767.0, 32767.0), e


def decoded(ref, rows):
    scale = jnp.exp2(ref[rows:rows + 1, :].astype(jnp.int32).astype(F32))
    return ref[0:rows, :].astype(jnp.int32).astype(F32) * scale


def kernel(strag, decode, enc_hbm, p_hbm, g_hbm, w_hbm, emb, out_ref,
           encode, g, p, gsib, psib, wt, t, q1, r1, s, s2, r2, u, s3, r3, msg, msgs,
           lsem, msem_s, msem_r, tsem_s, tsem_r, xsem_s, xsem_r, asem_s, asem_r, csem_s, csem_r, bsem_s, bsem_r,
           sem1_s, sem1_r, sem2_s, sem2_r, sem3_s, sem3_r):
    dp, fs = lax.axis_index("dp"), lax.axis_index("fsdp")
    core = lax.rem(dp, 2)
    xl = lax.rem(lax.div(dp, 2), X_LO)
    z = lax.div(dp, 2 * X_LO)
    xh = lax.div(fs, RING)
    y = lax.rem(fs, RING)
    x = xh * X_LO + xl

    def wrap(v):
        return lax.rem(v + RING, RING)

    def dev(x_, y_, z_, c_):
        return (z_ * 2 * X_LO + lax.rem(x_, X_LO) * 2 + c_, lax.div(x_, X_LO) * RING + y_)

    sib = (dp + 1 - 2 * core, fs)
    chip = lax.div(dp, 2)
    chips = 32
    following = lax.rem(chip + 1, chips)
    preceding = lax.rem(chip + chips - 1, chips)

    def remote(src, dst, ss, rs, to):
        return pltpu.make_async_remote_copy(src_ref=src, dst_ref=dst, send_sem=ss, recv_sem=rs,
                                            device_id=to, device_id_type=MESH)

    shard_rows = pl.ds(pl.multiple_of(fs * SHARD, SHARD), SHARD)
    def columns(h, c_):
        return pl.ds(pl.multiple_of(h * (DW // 2) + c_ * 2 * COLS, COLS), 2 * COLS)

    def load(src, dst, k):
        copy = pltpu.make_async_copy(src, dst, lsem.at[k])
        copy.start()
        return copy

    load_e = load(enc_hbm, encode, 0)
    load_w = load(w_hbm, wt.at[shard_rows], 1)
    load_p = load(p_hbm, p, 2)
    load_theirs = [load(g_hbm.at[:, columns(h, 1 - core)], g.at[:, columns(h, 1 - core)], 3 + h) for h in (0, 1)]
    load_mine = [load(g_hbm.at[:, columns(h, core)], g.at[:, columns(h, core)], 5 + h) for h in (0, 1)]

    barrier = pltpu.get_barrier_semaphore()
    partners = [sib]
    for k in (1, 2, RING - 2, RING - 1):
        partners.append(dev(lax.rem(x + k, RING), y, z, core))
        partners.append(dev(x, y, lax.rem(z + k, RING), core))
        partners.append(dev(x, lax.rem(y + k, RING), z, core))
    for other in (following, preceding):
        partners.append((2 * other, fs))
        partners.append((2 * other + 1, fs))
    for to in partners:
        pl.semaphore_signal(barrier, inc=1, device_id=to, device_id_type=MESH)

    load_e.wait()
    served = strag[0] * decode[0]
    row = lax.broadcasted_iota(jnp.int32, (8, 128), 0)
    msg[...] = jnp.where(row == 0, served * encode[0, 0], served * encode[0, 1])

    pl.semaphore_wait(barrier, len(partners))

    share_sib = remote(msg, msgs.at[0], msem_s.at[0], msem_r.at[0], sib)
    share_sib.start()
    share_next = [remote(msg, msgs.at[1], msem_s.at[1 + c], msem_r.at[1], (2 * following + c, fs)) for c in (0, 1)]

    @pl.when(core == 1)
    def _():
        for copy in share_next:
            copy.start()

    def unit(x_hi, y_, c_):
        return wt.at[pl.ds(pl.multiple_of((x_hi * RING + y_) * SHARD + c_ * HALF, 32), HALF)]

    def passed(block, k):
        return remote(block, block, bsem_s.at[k], bsem_r.at[k], sib)

    def own_at(way, hop, c_):
        return unit(xh, wrap(y - STEP[way] * hop), c_)

    def own_send(way, hop):
        block = own_at(way, hop, core)
        to = dev(x, wrap(y + STEP[way]), z, core)
        return remote(block, block, asem_s.at[way, hop], asem_r.at[way, hop], to)

    def own_pass(way, hop, c_):
        return passed(own_at(way, hop, c_), 4 * way + hop - 1)

    def own_hop(hop):
        for way in (PLUS, MINUS):
            if hop <= OWN_HOPS[way]:
                block = own_at(way, hop, core)
                remote(block, block, asem_s.at[way, hop - 1], asem_r.at[way, hop - 1], sib).wait_recv()
                if hop < OWN_HOPS[way]:
                    own_send(way, hop).start()
                own_pass(way, hop, core).start()

    def far_at(reach, c_):
        return unit(1 - xh, wrap(y - reach), c_)

    def far_send(k):
        reach = REACH[k]
        held = 0 if abs(reach) <= 2 else (2 if reach > 0 else -2)
        block = far_at(held, core)
        return remote(block, block, csem_s.at[k], csem_r.at[k], dev(x, wrap(y + reach - held), z, core))

    def far_pass(k, c_):
        return passed(far_at(REACH[k], c_), 8 + k)

    def far_arrive(k):
        block = far_at(REACH[k], core)
        remote(block, block, csem_s.at[k], csem_r.at[k], sib).wait_recv()

    load_w.wait()
    edge = (xl == 0) | (xl == X_LO - 1)
    outward = jnp.where(xl == 0, RING - 1, 1)
    own_unit = unit(xh, y, core)
    cross = [remote(own_unit, own_unit, xsem_s.at[k], xsem_r.at[0],
                    dev(lax.rem(x + (k + 1) * outward, RING), y, z, core)) for k in (0, 1)]

    @pl.when(edge)
    def _():
        for copy in cross:
            copy.start()

    for way in (PLUS, MINUS):
        own_send(way, 0).start()

    load_p.wait()
    tokens = [remote(p, psib, tsem_s.at[2], tsem_r.at[2], sib)]
    tokens[0].start()
    for h in (0, 1):
        load_theirs[h].wait()
        copy = remote(g.at[:, columns(h, 1 - core)], gsib.at[h], tsem_s.at[h], tsem_r.at[h], sib)
        copy.start()
        tokens.append(copy)
    for copy in load_mine:
        copy.wait()

    feature = lax.broadcasted_iota(jnp.int32, (P_SIZE, P_SIZE), 1)
    twelfth = jnp.right_shift(feature * 43691, 19)
    z_of = jnp.right_shift(feature * 10923, 19)
    place = (twelfth - X_LO * z_of) * PIECE + z_of * 12 + (feature - 12 * twelfth)
    out_row = lax.broadcasted_iota(jnp.int32, (P_SIZE, P_SIZE), 0)
    turn = (
        (out_row == feature).astype(F32).astype(BF16),
        (out_row == place).astype(F32).astype(BF16),
    )

    def features_first(q, tok):
        return lax.dot_general(turn[q], tok, (((1,), (1,)), ((), ())), preferred_element_type=F32).astype(BF16)

    for q in (0, 1):
        mine = features_first(q, p[...])
        for h in (0, 1):
            here = pl.ds(pl.multiple_of(h * (DW // 2) + core * 2 * COLS + q * COLS, COLS), COLS)
            term = jnp.dot(mine, g[:, here], preferred_element_type=F32)
            if q == 0:
                for k in range(RING):
                    t[0, k, h * PH:(h + 1) * PH, :] = term[k * PH:(k + 1) * PH]
            else:
                for k in range(X_LO):
                    t[1, h * X_LO + k, :, :] = term[k * PIECE:(k + 1) * PIECE]

    own_hop(1)
    crossed = far_at(0, core)
    remote(crossed, crossed, xsem_s.at[0], xsem_r.at[0], sib).wait_recv()
    for k in (1, 3, 0, 2):
        far_send(k).start()
    passed(crossed, 15).start()

    share_sib.wait_recv()
    remote(msg, msgs.at[1], msem_s.at[1], msem_r.at[1], sib).wait_recv()
    before = msgs[1, 1:2, 0:1]
    first_own, second_own = msg[0:1, 0:1], msg[1:2, 0:1]
    first_sib, second_sib = msgs[0, 0:1, 0:1], msgs[0, 1:2, 0:1]
    lower = core == 0
    scale_own = (first_own + jnp.where(lower, before, second_sib)).astype(F32) / (TOK * 16)
    scale_sib = (first_sib + jnp.where(lower, second_own, before)).astype(F32) / (TOK * 16)

    for copy in tokens:
        copy.wait_recv()

    pos = (z, x)

    def beside(q, v):
        return dev(x, y, v, core) if q == 0 else dev(v, y, z, core)

    turned = 1 - 2 * lax.rem(pos[0], 2), 1 - 2 * lax.rem(pos[1], 2)
    route = ((4, 2), (-3, -1), (3, 2), (-2, -1), (-1, -1), (2, 2), (1, 1))

    def along(q, k):
        slot = q1.at[q, k]
        return remote(slot, r1.at[q, k], sem1_s.at[q, k], sem1_r.at[q, k], beside(q, wrap(pos[q] + turned[q] * route[k][1])))

    def along_send(q, k):
        v = t[q, wrap(pos[q] + turned[q] * route[k][0])]
        for got in {5: (0, 1), 6: (2, 3)}.get(k, ()):
            along_wait(q, got)
            v += decoded(r1.at[q, got], PIECE)
        v, e = code(v)
        q1[q, k, 0:PIECE, :] = v.astype(jnp.int32).astype(I16)
        q1[q, k, PIECE:PIECE + SCALE, :] = jnp.broadcast_to(e, (SCALE, COLS)).astype(jnp.int32).astype(I16)
        along(q, k).start()

    def along_wait(q, k):
        slot = r1.at[q, k]
        remote(slot, slot, sem1_s.at[q, k], sem1_r.at[q, k], sib).wait_recv()

    for q in (0, 1):
        others = features_first(q, psib[...])
        for h in (0, 1):
            term = scale_sib * jnp.dot(others, gsib[h, :, q * COLS:(q + 1) * COLS], preferred_element_type=F32)
            if q == 0:
                for k in range(RING):
                    rows = slice(h * PH, (h + 1) * PH)
                    t[0, k, rows, :] = scale_own * t[0, k, rows, :] + term[k * PH:(k + 1) * PH]
            else:
                for k in range(X_LO):
                    at = h * X_LO + k
                    t[1, at, :, :] = scale_own * t[1, at, :, :] + term[k * PIECE:(k + 1) * PIECE]
        for k in range(5):
            along_send(q, k)

    own_hop(2)
    for k in (1, 3):
        far_arrive(k)
        for j in ((4, 5) if k == 1 else (6,)):
            far_send(j).start()
        far_pass(k, core).start()
    own_hop(3)
    for k in (5, 6):
        for q in (0, 1):
            along_send(q, k)
    own_hop(4)

    def embed_half(x_hi):
        def embed(j, carry):
            at = pl.multiple_of(x_hi * (DW // 2) + j * COLS, COLS)
            e = lax.dot_general(p[...], wt[pl.ds(at, COLS), :], (((1,), (1,)), ((), ())), preferred_element_type=F32)
            emb[:, pl.ds(at, COLS)] = e.astype(BF16)
            return carry

        lax.fori_loop(0, DW // 2 // COLS, embed, 0)

    for k in (0, 2, 4, 6, 5):
        far_arrive(k)
        far_pass(k, core).start()

    pos2 = (x, z)

    def across(q, j):
        k = wrap(pos2[q] + j - RING)
        return remote(s2.at[q, k], r2.at[q, j], sem2_s.at[q, j], sem2_r.at[q, j], beside(1 - q, k))

    for q in (0, 1):
        for k in (4, 5, 6):
            along_wait(q, k)
        total = t[q, pos[q]]
        for k in (4, 5, 6):
            total += decoded(r1.at[q, k], PIECE)
        s[q, 0:PIECE, :] = total
        s[q, PIECE:PIECE + 8, :] = jnp.zeros((8, COLS), F32)
    data_row = lax.broadcasted_iota(jnp.int32, (RING, 16, COLS), 1) < 12
    for q in (0, 1):
        v = jnp.stack([s[q, 12 * k:12 * k + 16, :] for k in range(RING)])
        v, e = code(jnp.where(data_row, v, 0.0), 1)
        s2[q] = jnp.where(data_row, v, e).astype(jnp.int32).astype(I16)
        for j in range(1, RING):
            across(q, j).start()

    for way in (PLUS, MINUS):
        for hop in range(1, OWN_HOPS[way] + 1):
            own_pass(way, hop, 1 - core).wait_recv()
    embed_half(xh)

    for k in range(7):
        far_pass(k, 1 - core).wait_recv()
    passed(far_at(0, 1 - core), 15).wait_recv()
    embed_half(1 - xh)

    def onward(q, par, c_):
        y_to = 4 * core + 2 * q + par
        return y_to, remote(s3.at[q, par, c_], r3.at[y], sem3_s.at[q, par, c_], sem3_r.at[y], dev(x, y_to, z, c_))

    for q in (0, 1):
        for j in range(1, RING):
            across(q, j).wait_recv()
        total = decoded(s2.at[q, pos2[q]], 12)
        for j in range(1, RING):
            total += decoded(r2.at[q, j], 12)
        u[q, 0:12, :] = total
        u[q, 12:16, :] = jnp.zeros((4, COLS), F32)
        for par in (0, 1):
            for c_ in (0, 1):
                s3[q, par, c_] = u[q, 6 * c_:6 * c_ + 8, par * SHARD:(par + 1) * SHARD]
                y_to, copy = onward(q, par, c_)
                self_ = (y_to == y) & (core == c_)

                @pl.when(self_)
                def _():
                    r3[y] = s3[q, par, c_]

                @pl.when(jnp.logical_not(self_))
                def _():
                    copy.start()

    summed_by = lax.div(y, 4)
    for k in range(RING):
        slot = r3.at[k]

        @pl.when(jnp.logical_not((y == k) & (core == summed_by)))
        def _():
            remote(slot, slot, sem3_s.at[0, 0, 0], sem3_r.at[k], sib).wait_recv()

    total = r3[0]
    for k in range(1, RING):
        total += r3[k]
    out_ref[...] = total[0:6]

    share_sib.wait_send()

    @pl.when(core == 1)
    def _():
        for copy in share_next:
            copy.wait_send()

    @pl.when(edge)
    def _():
        for copy in cross:
            copy.wait_send()

    for copy in tokens:
        copy.wait_send()
    passed(crossed, 15).wait_send()
    for way in (PLUS, MINUS):
        for hop in range(OWN_HOPS[way]):
            own_send(way, hop).wait_send()
            own_pass(way, hop + 1, core).wait_send()
    for k in range(7):
        far_send(k).wait_send()
        far_pass(k, core).wait_send()
        for q in (0, 1):
            along(q, k).wait_send()
    for q in (0, 1):
        for j in range(1, RING):
            across(q, j).wait_send()
        for par in (0, 1):
            for c_ in (0, 1):
                y_to, copy = onward(q, par, c_)

                @pl.when(jnp.logical_not((y_to == y) & (core == c_)))
                def _():
                    copy.wait_send()


def body(patches, grad_embed, weight, straggler, decode, encode):
    hbm = pl.BlockSpec(memory_space=pltpu.HBM)
    vmem = pl.BlockSpec(memory_space=pltpu.VMEM)
    smem = pl.BlockSpec(memory_space=pltpu.SMEM)
    dma = pltpu.SemaphoreType.DMA
    return pl.pallas_call(
        kernel,
        out_shape=(
            pltpu.VMEM((TOK, DW), BF16),
            pltpu.VMEM((6, SHARD), F32),
        ),
        in_specs=[smem] * 2 + [hbm] * 4,
        out_specs=(vmem, vmem),
        scratch_shapes=[
            pltpu.SMEM((1, 2), jnp.int32),
            pltpu.VMEM((TOK, DW), BF16),
            pltpu.VMEM((TOK, P_SIZE), BF16),
            pltpu.VMEM((2, TOK, 2 * COLS), BF16),
            pltpu.VMEM((TOK, P_SIZE), BF16),
            pltpu.VMEM((DW, P_SIZE), BF16),
            pltpu.VMEM((2, RING, PIECE, COLS), F32),
            pltpu.VMEM((2, 7, PIECE + SCALE, COLS), I16),
            pltpu.VMEM((2, 7, PIECE + SCALE, COLS), I16),
            pltpu.VMEM((2, PIECE + 8, COLS), F32),
            pltpu.VMEM((2, RING, 16, COLS), I16),
            pltpu.VMEM((2, RING, 16, COLS), I16),
            pltpu.VMEM((2, 16, COLS), F32),
            pltpu.VMEM((2, 2, 2, 8, SHARD), F32),
            pltpu.VMEM((RING, 8, SHARD), F32),
            pltpu.VMEM((8, 128), jnp.int32),
            pltpu.VMEM((2, 8, 128), jnp.int32),
            dma((7,)),
            dma((3,)), dma((2,)),
            dma((3,)), dma((3,)),
            dma((2,)), dma((1,)),
            dma((2, 4)), dma((2, 4)),
            dma((7,)), dma((7,)),
            dma((16,)), dma((16,)),
            dma((2, 7)), dma((2, 7)),
            dma((2, RING)), dma((2, RING)),
            dma((2, 2, 2)), dma((RING,)),
        ],
        compiler_params=pltpu.CompilerParams(
            collective_id=0, has_side_effects=True, vmem_limit_bytes=48 * 1024 * 1024
        ),
    )(straggler, decode, *(pltpu.with_memory_space_constraint(v, pltpu.HBM) for v in (encode, patches, grad_embed, weight.T)))


def solution(mesh):
    return jax.shard_map(
        body,
        mesh=mesh,
        in_specs=(
            P(("dp", "fsdp"), None),
            P(("dp", "fsdp"), None),
            P(None, "fsdp"),
            P("dp"),
            P("dp"),
            P("dp", None),
        ),
        out_specs=(P(("dp", "fsdp"), None), P("dp", "fsdp")),
        check_vma=False,
    )
```

time: 59.7 us -> 57.8 us (0.968)
  Pallas kernels: 55.8 us -> 54 us
    pallas_call x1, Pallas kernels: 55.8 us -> 54 us  [body(): pl.pallas_call(kernel, out_shape=(pltpu.VMEM((TOK, DW), BF16), pltpu.VMEM...]
where the time goes in v3:
time: 57.8 us; the launch traced here: 57.7 us
  Pallas kernels  54 us (93%)
  between operations  1.93 us (3%)
  local copies, waits for them, and re-layouts  1.74 us (3%)
    pallas_call x1, Pallas kernels, body(): pl.pallas_call(kernel, out_shape=(pltpu.VMEM((TOK, DW), BF16), pltpu.VMEM...  54 us
    unnamed x2, local copies, waits for them, and re-layouts  1.74 us

profile of v3, /device:TPU:1, one launch (start us, length us, event | category | flops | bytes accessed | tf_op | source)
XLA Modules:
  0.0 57.7 jit_solution(13883141218255655394)
XLA Ops:
  1.9 54.0 %shard_map.77 = (bf16[256,3072]{1,0:T(8,128)(2,1)S(1)}, f32[6,192]{1,0:T(8,128)S(1)}) custom-call(s32[1]{0:T(128)S(6)} %copy.12.strag, s32[1]{0:T(128)S(6)} %copy.13.decode, s32[1,2]{1,0:T(1,128)} %enc_hbm.1, bf16[256,384]{1,0:T(8,128)(2,1)} %p_hbm.1, bf16[256,3072]{1,0:T(8,128)(2,1)} %g_hbm.1, bf16[192,384]{1,0:T(8,128)(2,1)} %bitcast.1), custom_call_target="tpu_custom_call" | custom-call | tf_op jit(solution)/shard_map/pallas_call | solution.py:406
  55.9 1.1 %copy.10 = bf16[256,3072]{1,0:T(8,128)(2,1)} copy(bf16[256,3072]{1,0:T(8,128)(2,1)S(1)} %get-tuple-element.2) | data formatting | bytes 3145728
  57.1 0.6 %copy.11 = f32[6,192]{1,0:T(8,128)} copy(f32[6,192]{1,0:T(8,128)S(1)} %get-tuple-element.3) | data formatting | bytes 9216

commit v4 on v3

--- a/solution.py
+++ b/solution.py
@@ -32,9 +32,13 @@
     return jnp.floor(jnp.log2(jnp.maximum(top, 2.0 ** -100))) - 14.0
 
 
+def rounded(v, e):
+    return jnp.clip(jnp.round(v * jnp.exp2(-e)), -32767.0, 32767.0)
+
+
 def code(v, over=0):
     e = scales(jnp.max(jnp.abs(v), axis=over, keepdims=True))
-    return jnp.clip(jnp.round(v * jnp.exp2(-e)), -32767.0, 32767.0), e
+    return rounded(v, e), e
 
 
 def decoded(ref, rows):
@@ -43,7 +47,7 @@
 
 
 def kernel(strag, decode, enc_hbm, p_hbm, g_hbm, w_hbm, emb, out_ref,
-           encode, g, p, gsib, psib, wt, t, q1, r1, s, s2, r2, u, s3, r3, msg, msgs,
+           encode, g, p, gsib, psib, wt, t, ex, q1, r1, s, s2, r2, u, s3, r3, msg, msgs,
            lsem, msem_s, msem_r, tsem_s, tsem_r, xsem_s, xsem_r, asem_s, asem_r, csem_s, csem_r, bsem_s, bsem_r,
            sem1_s, sem1_r, sem2_s, sem2_r, sem3_s, sem3_r):
     dp, fs = lax.axis_index("dp"), lax.axis_index("fsdp")
@@ -238,11 +242,12 @@
         return remote(slot, r1.at[q, k], sem1_s.at[q, k], sem1_r.at[q, k], beside(q, wrap(pos[q] + turned[q] * route[k][1])))
 
     def along_send(q, k):
-        v = t[q, wrap(pos[q] + turned[q] * route[k][0])]
+        piece = wrap(pos[q] + turned[q] * route[k][0])
+        v = t[q, piece]
         for got in {5: (0, 1), 6: (2, 3)}.get(k, ()):
             along_wait(q, got)
             v += decoded(r1.at[q, got], PIECE)
-        v, e = code(v)
+        v, e = code(v) if k > 4 else (rounded(v, ex[q, piece, 0:1, :]), ex[q, piece, 0:1, :])
         q1[q, k, 0:PIECE, :] = v.astype(jnp.int32).astype(I16)
         q1[q, k, PIECE:PIECE + SCALE, :] = jnp.broadcast_to(e, (SCALE, COLS)).astype(jnp.int32).astype(I16)
         along(q, k).start()
@@ -263,6 +268,8 @@
                 for k in range(X_LO):
                     at = h * X_LO + k
                     t[1, at, :, :] = scale_own * t[1, at, :, :] + term[k * PIECE:(k + 1) * PIECE]
+        tops = jnp.max(jnp.abs(t[q]), axis=1, keepdims=True)
+        ex[q] = jnp.broadcast_to(scales(tops), (RING, SCALE, COLS))
         for k in range(5):
             along_send(q, k)
 
@@ -317,11 +324,6 @@
         for hop in range(1, OWN_HOPS[way] + 1):
             own_pass(way, hop, 1 - core).wait_recv()
     embed_half(xh)
-
-    for k in range(7):
-        far_pass(k, 1 - core).wait_recv()
-    passed(far_at(0, 1 - core), 15).wait_recv()
-    embed_half(1 - xh)
 
     def onward(q, par, c_):
         y_to = 4 * core + 2 * q + par
@@ -348,6 +350,11 @@
                 @pl.when(jnp.logical_not(self_))
                 def _():
                     copy.start()
+
+    for k in range(7):
+        far_pass(k, 1 - core).wait_recv()
+    passed(far_at(0, 1 - core), 15).wait_recv()
+    embed_half(1 - xh)
 
     summed_by = lax.div(y, 4)
     for k in range(RING):
@@ -419,6 +426,7 @@
             pltpu.VMEM((TOK, P_SIZE), BF16),
             pltpu.VMEM((DW, P_SIZE), BF16),
             pltpu.VMEM((2, RING, PIECE, COLS), F32),
+            pltpu.VMEM((2, RING, SCALE, COLS), F32),
             pltpu.VMEM((2, 7, PIECE + SCALE, COLS), I16),
             pltpu.VMEM((2, 7, PIECE + SCALE, COLS), I16),
             pltpu.VMEM((2, PIECE + 8, COLS), F32),

time: 57.8 us -> 57.9 us (level)
  no operation moved by 1% of the time
where the time goes in v4:
time: 57.9 us; the launch traced here: 57.7 us
  Pallas kernels  54 us (93%)
  between operations  1.93 us (3%)
  local copies, waits for them, and re-layouts  1.74 us (3%)
    pallas_call x1, Pallas kernels, body(): pl.pallas_call(kernel, out_shape=(pltpu.VMEM((TOK, DW), BF16), pltpu.VMEM...  54 us
    unnamed x2, local copies, waits for them, and re-layouts  1.74 us

profile of v4, /device:TPU:1, one launch (start us, length us, event | category | flops | bytes accessed | tf_op | source)
XLA Modules:
  0.0 57.7 jit_solution(13184919658603901091)
XLA Ops:
  1.9 54.0 %shard_map.77 = (bf16[256,3072]{1,0:T(8,128)(2,1)S(1)}, f32[6,192]{1,0:T(8,128)S(1)}) custom-call(s32[1]{0:T(128)S(6)} %copy.12.strag, s32[1]{0:T(128)S(6)} %copy.13.decode, s32[1,2]{1,0:T(1,128)} %enc_hbm.1, bf16[256,384]{1,0:T(8,128)(2,1)} %p_hbm.1, bf16[256,3072]{1,0:T(8,128)(2,1)} %g_hbm.1, bf16[192,384]{1,0:T(8,128)(2,1)} %bitcast.1), custom_call_target="tpu_custom_call" | custom-call | tf_op jit(solution)/shard_map/pallas_call | solution.py:413
  55.9 1.1 %copy.10 = bf16[256,3072]{1,0:T(8,128)(2,1)} copy(bf16[256,3072]{1,0:T(8,128)(2,1)S(1)} %get-tuple-element.2) | data formatting | bytes 3145728
  57.1 0.6 %copy.11 = f32[6,192]{1,0:T(8,128)} copy(f32[6,192]{1,0:T(8,128)S(1)} %get-tuple-element.3) | data formatting | bytes 9216
